TPU v7x, 512 devices: a whole 4x8x8 slice. The times are simulated.
512 devices in a mesh: brow: 32 (over z_lo, y, core), bcol: 16 (over z_hi, x).
Axes of the slice: x: 4, y: 8, z: 8 (z_hi: 4, z_lo: 2; z = z_hi * 2 + z_lo), core: 2. Of those that a mesh axis runs over, the one named last changes fastest.
Arguments:
- vectors: bfloat16 [8, 1048576], P(None, ('brow', 'bcol')), may hold values from -6 to 6
- tiles: bfloat16 [98304, 4096], P(('brow', 'bcol')), may hold values from -0.29882812 to 0.29882812
- tile_rows: int32 [98304], P(('brow', 'bcol')), may hold values from 0 to 511
- tile_cols: int32 [98304], P(('brow', 'bcol')), may hold values from 0 to 1023
- counts: int32 [32, 16], P('brow', 'bcol'), may hold values from 64 to 192, as said below
Outputs:
- product: float32 [8, 1048576], P(None, ('brow', 'bcol'))
Inputs may be any that keep to these rules, and one draw needn't show every extreme that they name: `counts`: some grid block uses all 192 slots in every draw; every block uses at least a third of them.
All inputs are finite; a program needn't handle non-finite values.
Results may differ from a plain program's by a relative error of at most 0.0003.
Values may be sent and summed in bfloat16 or wider, within the bound.
A program may use at most 64 MiB of HBM per device.

v0:
```python
import jax
import jax.numpy as jnp
from jax import lax
from jax.sharding import PartitionSpec as P

TILE = 64


def body(vectors, tiles, tile_rows, tile_cols, counts):
    width = vectors.shape[0]
    piece = vectors.shape[1]
    slots = tiles.shape[0]
    side = TILE
    n_rows_axis = lax.axis_size("brow")
    n_cols_axis = lax.axis_size("bcol")
    row_tiles = piece * n_cols_axis // side
    col_tiles = piece * n_rows_axis // side
    live = (jnp.arange(slots, dtype=jnp.int32) < counts[0, 0]).astype(jnp.bfloat16)
    row_hot = (tile_rows[:, None] == jnp.arange(row_tiles, dtype=jnp.int32)[None, :]).astype(
        jnp.bfloat16
    ) * live[:, None]
    col_hot = (tile_cols[:, None] == jnp.arange(col_tiles, dtype=jnp.int32)[None, :]).astype(
        jnp.bfloat16
    ) * live[:, None]
    row_hot_wide = row_hot.astype(jnp.float32)
    col_hot_wide = col_hot.astype(jnp.float32)
    blocks = tiles.reshape(slots, side, side)
    col_seg = lax.all_gather(vectors, "brow", axis=1, tiled=True).reshape(width, col_tiles, side)
    at_cols = jnp.einsum(
        "tc,kcj->tkj", col_hot, col_seg, preferred_element_type=jnp.float32
    ).astype(jnp.bfloat16)
    forward = jnp.einsum("tkj,tij->tki", at_cols, blocks, preferred_element_type=jnp.float32)
    partial_rows = jnp.einsum("tr,tki->kri", row_hot_wide, forward, precision=lax.Precision.HIGHEST)
    partial_rows = partial_rows.reshape(width, row_tiles * side)
    from_rows = lax.psum_scatter(partial_rows, "bcol", scatter_dimension=1, tiled=True)
    row_seg = lax.all_gather(vectors, "bcol", axis=1, tiled=True).reshape(width, row_tiles, side)
    at_rows = jnp.einsum(
        "tr,kri->tki", row_hot, row_seg, preferred_element_type=jnp.float32
    ).astype(jnp.bfloat16)
    backward = jnp.einsum("tki,tij->tkj", at_rows, blocks, preferred_element_type=jnp.float32)
    partial_cols = jnp.einsum(
        "tc,tkj->kcj", col_hot_wide, backward, precision=lax.Precision.HIGHEST
    )
    partial_cols = partial_cols.reshape(width, col_tiles * side)
    from_cols = lax.psum_scatter(partial_cols, "brow", scatter_dimension=1, tiled=True)
    return from_rows + from_cols


def solution(mesh):
    return jax.shard_map(
        body,
        mesh=mesh,
        in_specs=(
            P(None, ("brow", "bcol")),
            P(("brow", "bcol"), None),
            P(("brow", "bcol")),
            P(("brow", "bcol")),
            P("brow", "bcol"),
        ),
        out_specs=P(None, ("brow", "bcol")),
        check_vma=False,
    )
```

profile of v0, /device:TPU:6, one launch (start us, length us, event | category | flops | bytes accessed | tf_op | source)
XLA Modules:
  0.0 323.2 jit_solution(9489676851828670037)
XLA Ops:
  6.5 0.0 all-gather.2.cloned.1.call-start
  6.5 0.7 all-gather.2.cloned.1.call-update
  7.3 0.0 reduce-scatter.3.cloned.1.call-start
  7.9 3.9 %copy.6 = bf16[192,4096]{0,1:T(8,128)(2,1)} copy(bf16[192,4096]{1,0:T(8,128)(2,1)} %param.6) | data formatting | bytes 3145728 | tf_op args[1]
  11.8 4.2 %copy.13 = bf16[192,64,64]{2,1,0:T(8,128)(2,1)S(1)} copy(bf16[192,64,64]{0,2,1:T(8,128)(2,1)} %bitcast.21) | data formatting | bytes 3145728 | tf_op jit(solution)/shard_map/reshape | solution.py:27
  16.0 0.0 copy-start.2
  16.1 64.3 %all-gather.2.cloned.1.call-done = bf16[8,65536]{1,0:T(8,128)(2,1)} async-done(((bf16[8,2048]{1,0:T(8,128)(2,1)}), bf16[8,65536]{1,0:T(8,128)(2,1)}) %all-gather.2.cloned.1.call-update) | async-done | bytes 1048592 | tf_op jit(solution)/shard_map/all_gather | solution.py:28
  80.4 4.5 %reshape.22 = bf16[8,1024,64]{2,1,0:T(8,128)(2,1)} reshape(bf16[8,65536]{1,0:T(8,128)(2,1)} %all-gather.2.cloned.1.call-done) | data formatting | bytes 2097152 | tf_op jit(solution)/shard_map/reshape | solution.py:28
  84.9 0.0 copy-done.2
  84.9 3.2 fusion.5
  88.0 1.2 copy.9
  89.2 0.0 copy-start.1
  89.2 1.7 fusion.33
  91.0 0.0 copy-done.1
  91.0 2.0 convolution_bitcast_fusion.1
  92.9 3.2 copy.7
  96.1 0.0 copy-start
  96.1 3.2 %reshape.24 = f32[8,32768]{1,0:T(8,128)} reshape(f32[8,512,64]{2,1,0:T(8,128)} %copy.7) | data formatting | bytes 2097152 | tf_op jit(solution)/shard_map/reshape | solution.py:34
  99.3 0.0 reduce-scatter.3.cloned.1.call-update
  99.4 0.0 reduce-scatter.5.cloned.1.call-start
  99.4 0.0 copy-done
  99.4 40.4 %all_gather.7 = bf16[8,32768]{1,0:T(8,128)(2,1)} all-gather(bf16[8,2048]{1,0:T(8,128)(2,1)S(1)} %copy-done), channel_id=1, replica_groups=mesh['brow'=32,'bcol'=16] {'bcol'}, dimensions={1}, use_global_device_ids=true | all-gather | bytes 557056 | tf_op jit(solution)/shard_map/all_gather | solution.py:36
  139.9 3.0 reshape.25
  142.9 2.5 fusion.15
  145.4 1.2 copy.12
  146.6 0.9 fusion.32
  147.5 1.2 convolution_bitcast_fusion
  148.7 2.7 copy.8
  151.4 4.8 %reshape.26 = f32[8,65536]{1,0:T(8,128)} reshape(f32[8,1024,64]{2,1,0:T(8,128)} %copy.8) | data formatting | bytes 4194304 | tf_op jit(solution)/shard_map/reshape | solution.py:44
  156.2 0.0 reduce-scatter.5.cloned.1.call-update
  156.2 36.0 %reduce-scatter.3.cloned.1.call-done = f32[8,2048]{1,0:T(8,128)} async-done(((f32[8,32768]{1,0:T(8,128)}), f32[8,2048]{1,0:T(8,128)}) %reduce-scatter.3.cloned.1.call-update) | async-done | bytes 65552 | tf_op jit(solution)/shard_map/reduce_scatter | solution.py:35
  192.2 123.0 %reduce-scatter.5.cloned.1.call-done = f32[8,2048]{1,0:T(8,128)} async-done(((f32[8,65536]{1,0:T(8,128)}), f32[8,2048]{1,0:T(8,128)}) %reduce-scatter.5.cloned.1.call-update) | async-done | bytes 65552 | tf_op jit(solution)/shard_map/reduce_scatter | solution.py:45
  315.2 1.5 add.7
  (1 shorter events, 0.0 us)
Async XLA Ops:
  6.5 73.8 %all-gather.2.cloned.1.call-start = ((), (), s32[]{:S(2)}) async-start(), calls=%async_computation.2 | async-start | bytes 1081344 | tf_op jit(solution)/shard_map/all_gather | solution.py:28
  7.3 184.9 %reduce-scatter.3.cloned.1.call-start = ((), (), s32[]{:S(2)}) async-start(), calls=%async_computation.3 | async-start | bytes 1114112 | tf_op jit(solution)/shard_map/reduce_scatter | solution.py:35
  16.0 68.9 %copy-start.2 = (s32[192]{0:T(256)S(1)}, s32[192]{0:T(256)}, u32[]{:S(2)}) copy-start(s32[192]{0:T(256)} %param.8) | copy-start | bytes 2308
  89.2 1.7 copy-start.1
  96.1 3.3 %copy-start = (bf16[8,2048]{1,0:T(8,128)(2,1)S(1)}, bf16[8,2048]{1,0:T(8,128)(2,1)}, u32[]{:S(2)}) copy-start(bf16[8,2048]{1,0:T(8,128)(2,1)} %param.5) | copy-start | bytes 98308
  99.4 215.8 %reduce-scatter.5.cloned.1.call-start = ((), (), s32[]{:S(2)}) async-start(), calls=%async_computation.4 | async-start | bytes 2162688 | tf_op jit(solution)/shard_map/reduce_scatter | solution.py:45
Sparse Core Ops, SparseCore 0:
  9.5 70.8 all-gather.1
  99.5 92.6 reduce-scatter.2
  195.0 120.1 reduce-scatter.4
where the time goes:
time: 324 us; the launch traced here: 323 us
  waiting for transfers between devices  224 us (69%)
  blocking collectives  40.4 us (12%)
  local copies, waits for them, and re-layouts  31.9 us (10%)
  between operations  13.8 us (4%)
  matrix products  11.4 us (4%)
    reduce_scatter x1, waiting for transfers between devices, body(): lax.psum_scatter(partial_cols, 'brow', scatter_dimension=1, tiled=True)  123 us
    all_gather x1, waiting for transfers between devices, body(): lax.all_gather(vectors, 'brow', axis=1, tiled=True)  64.3 us
    all_gather x1, blocking collectives, body(): lax.all_gather(vectors, 'bcol', axis=1, tiled=True)  40.4 us
    reduce_scatter x1, waiting for transfers between devices, body(): lax.psum_scatter(partial_rows, 'bcol', scatter_dimension=1, tiled=True)  36 us
  transfers between devices with their start and end apart: 3, of which 3 were waited for; matrix products, arithmetic and copies ran while one was open for 8% of the time, Pallas kernels for 0%

commit v1 on v0

v1 whole, which is shorter than its diff:
```python
import functools

import jax
import jax.numpy as jnp
from jax import lax
from jax.experimental import pallas as pl
from jax.experimental.pallas import tpu as pltpu
from jax.sharding import PartitionSpec as P

MESH = pl.DeviceIdType.MESH
TILE = 64
PIECE = 2048
SLOTS = 192
VECS = 8
NY, NX, NZH = 8, 4, 4
ROWS, COLS = 32, 16
GROUP = 16


def place():
    r = lax.axis_index("brow")
    c = lax.axis_index("bcol")
    return r, c, r // 16, (r // 2) % NY, r % 2, c // NX, c % NX


def row_id(zl, y, core):
    return zl * 16 + y * 2 + core


def remote(src, dst, send, recv, **where):
    return pltpu.make_async_remote_copy(
        src_ref=src, dst_ref=dst, send_sem=send, recv_sem=recv, device_id=where, device_id_type=MESH
    )


def greet(r, c, zl, y, core, zh, x):
    barrier = pltpu.get_barrier_semaphore()

    def call(**where):
        pl.semaphore_signal(barrier, inc=1, device_id=where, device_id_type=MESH)

    for d in (4, 3, 5, 2, 6, 1, 7):
        call(brow=row_id(zl, (y + d) % NY, core))
    for d in (2, 1, 3):
        call(bcol=((zh + d) % NZH) * NX + x)
    for d in (2, 1, 3):
        call(bcol=zh * NX + (x + d) % NX)
    call(brow=row_id(1 - zl, y, core))
    call(brow=row_id(zl, y, 1 - core))
    pl.semaphore_wait(barrier, 15)


def prep_kernel(tiles_ref, out_ref, flat, woven):
    lane = lax.broadcasted_iota(jnp.int32, (32, 128), 1)
    for b in range(32):
        flat[b * GROUP : (b + 1) * GROUP, :] = tiles_ref[:, b * 128 : (b + 1) * 128].astype(jnp.float32)
    for s in range(GROUP):
        m = flat[pl.ds(s, 32, stride=GROUP), :]
        turned = pltpu.roll(m, 64, 1)
        woven[pl.ds(s * TILE, 32, stride=2), :] = jnp.where(lane < 64, m, turned)
        woven[pl.ds(s * TILE + 1, 32, stride=2), :] = jnp.where(lane < 64, turned, m)
    for s in range(GROUP):
        out_ref[s] = woven[s * TILE : (s + 1) * TILE, :].astype(jnp.bfloat16)


def prep(tiles):
    return pl.pallas_call(
        prep_kernel,
        name="prep",
        grid=(SLOTS // GROUP,),
        in_specs=[pl.BlockSpec((GROUP, TILE * TILE), lambda g: (g, 0))],
        out_specs=pl.BlockSpec((GROUP, TILE, 128), lambda g: (g, 0, 0)),
        out_shape=jax.ShapeDtypeStruct((SLOTS, TILE, 128), jnp.bfloat16),
        scratch_shapes=[
            pltpu.VMEM((32 * GROUP, 128), jnp.float32),
            pltpu.VMEM((TILE * GROUP, 128), jnp.float32),
        ],
    )(tiles)


def gather_kernel(vec, col, row, col_send, col_recv, pass_send, near_send, row_send, row_recv, side_send, own_sem):
    r, c, zl, y, core, zh, x = place()
    z_mate = row_id(1 - zl, y, core)
    core_mate = row_id(zl, y, 1 - core)
    greet(r, c, zl, y, core, zh, x)
    sent = []

    def go(copy):
        copy.start()
        sent.append(copy)

    def arrived(buf, sems, index):
        remote(buf.at[index], buf.at[index], own_sem.at[0], sems.at[index], brow=core_mate).wait_recv()

    for n, d in enumerate((4, 3, 5, 2, 6, 1, 7)):
        go(remote(vec, col.at[r], col_send.at[n], col_recv.at[r], brow=row_id(zl, (y + d) % NY, core)))
    for n, d in enumerate((2, 1, 3)):
        go(remote(vec, row.at[c], row_send.at[n], row_recv.at[c], bcol=((zh + d) % NZH) * NX + x))
    go(remote(vec, col.at[r], pass_send.at[0], col_recv.at[r], brow=z_mate))
    for n, d in enumerate((2, 1, 3)):
        go(remote(vec, row.at[c], side_send.at[n], row_recv.at[c], bcol=zh * NX + (x + d) % NX))
    go(remote(vec, col.at[r], near_send.at[0], col_recv.at[r], brow=core_mate))
    mine = [
        pltpu.make_async_copy(vec, col.at[r], own_sem.at[1]),
        pltpu.make_async_copy(vec, row.at[c], own_sem.at[2]),
    ]
    for copy in mine:
        copy.start()

    def forward_y(n, d):
        src = row_id(zl, (y + d) % NY, core)
        arrived(col, col_recv, src)
        go(remote(col.at[src], col.at[src], pass_send.at[n], col_recv.at[src], brow=z_mate))
        go(remote(col.at[src], col.at[src], near_send.at[n], col_recv.at[src], brow=core_mate))

    def forward_zh(n, d):
        src = ((zh + d) % NZH) * NX + x
        arrived(row, row_recv, src)
        for m, e in enumerate((2, 1, 3)):
            go(
                remote(
                    row.at[src], row.at[src], side_send.at[3 * n + m], row_recv.at[src], bcol=zh * NX + (x + e) % NX
                )
            )

    def forward_z(n, d):
        src = row_id(1 - zl, (y + d) % NY, core)
        arrived(col, col_recv, src)
        go(remote(col.at[src], col.at[src], near_send.at[n], col_recv.at[src], brow=core_mate))

    forward_y(1, 1)
    forward_y(2, 7)
    forward_zh(1, 1)
    forward_zh(2, 3)
    forward_y(3, 2)
    forward_y(4, 6)
    forward_z(8, 0)
    forward_zh(3, 2)
    forward_y(5, 3)
    forward_y(6, 5)
    forward_z(9, 1)
    forward_z(10, 7)
    forward_y(7, 4)
    forward_z(11, 2)
    forward_z(12, 6)
    forward_z(13, 3)
    forward_z(14, 5)
    forward_z(15, 4)
    for copy in mine:
        copy.wait()
    for z in (0, 1):
        for d in range(NY):
            arrived(col, col_recv, row_id((zl + z) % 2, (y + d) % NY, 1 - core))
    for d in range(NZH):
        for e in (1, 2, 3):
            arrived(row, row_recv, ((zh + d) % NZH) * NX + (x + e) % NX)
    for copy in sent:
        copy.wait_send()


def gather(vectors):
    vmem = pl.BlockSpec(memory_space=pltpu.VMEM)
    dma = pltpu.SemaphoreType.DMA
    return pl.pallas_call(
        gather_kernel,
        name="gather",
        in_specs=[vmem],
        out_specs=[vmem, vmem],
        out_shape=[
            jax.ShapeDtypeStruct((ROWS, VECS, PIECE), jnp.bfloat16),
            jax.ShapeDtypeStruct((COLS, VECS, PIECE), jnp.bfloat16),
        ],
        scratch_shapes=[dma((7,)), dma((ROWS,)), dma((8,)), dma((16,)), dma((3,)), dma((COLS,)), dma((12,)), dma((3,))],
        compiler_params=pltpu.CompilerParams(collective_id=0, has_side_effects=True),
    )(vectors)


def apply_kernel(rows, cols, counts, tt, col, row, prow, pcol):
    n = counts[0, 0]
    prow[...] = jnp.zeros_like(prow)
    pcol[...] = jnp.zeros_like(pcol)
    high = (lax.broadcasted_iota(jnp.int32, (VECS, 128), 1) >= TILE).astype(jnp.int32)

    def spot(index):
        return index // 32, pl.ds(pl.multiple_of(((index // 2) % 16) * 128, 128), 128), index % 2

    def step(g, carry):
        done = []
        for u in range(8):
            s = g * 8 + u
            a, b = spot(rows[s]), spot(cols[s])
            live = (s < n).astype(jnp.int32)
            mask_a, mask_b = high == a[2], high == b[2]
            t = tt[s]
            w = jnp.concatenate([t, t], axis=0)
            xb = jnp.where(high == b[2] + 2 * (1 - live), col[b[0], :, b[1]].astype(jnp.float32), 0.0)
            xa = jnp.where(high == a[2] + 2 * (1 - live), row[a[0], :, a[1]].astype(jnp.float32), 0.0)
            fwd = lax.dot_general(
                xb.astype(jnp.bfloat16), w, (((1,), (1,)), ((), ())), preferred_element_type=jnp.float32
            )
            bwd = lax.dot_general(
                xa.astype(jnp.bfloat16), w, (((1,), (0,)), ((), ())), preferred_element_type=jnp.float32
            )
            done.append((a, b, jnp.where(mask_a, fwd, 0.0), jnp.where(mask_b, bwd, 0.0)))
        for a, b, fwd, bwd in done:
            prow[a[0], :, a[1]] += fwd
            pcol[b[0], :, b[1]] += bwd
        return carry

    lax.fori_loop(0, (n + 7) // 8, step, 0)


def apply(tile_rows, tile_cols, counts, tt, col, row):
    vmem = pl.BlockSpec(memory_space=pltpu.VMEM)
    smem = pl.BlockSpec(memory_space=pltpu.SMEM)
    return pl.pallas_call(
        apply_kernel,
        name="apply",
        in_specs=[smem, smem, smem, vmem, vmem, vmem],
        out_specs=[vmem, vmem],
        out_shape=[
            jax.ShapeDtypeStruct((COLS, VECS, PIECE), jnp.float32),
            jax.ShapeDtypeStruct((ROWS, VECS, PIECE), jnp.float32),
        ],
    )(tile_rows, tile_cols, counts, tt, col, row)


def scatter_kernel(
    prow, pcol, out, near_buf, near_sum, pass_buf, pass_sum, far_buf, side_buf, side_sum, hi_buf,
    near_send, near_recv, pass_send, pass_recv, far_send, far_recv, side_send, side_recv, hi_send, hi_recv,
):
    r, c, zl, y, core, zh, x = place()
    z_mate = row_id(1 - zl, y, core)
    core_mate = row_id(zl, y, 1 - core)
    greet(r, c, zl, y, core, zh, x)
    sent = []

    def go(copy):
        copy.start()
        sent.append(copy)

    def arrived(buf, sems, index):
        remote(buf.at[index], buf.at[index], near_send.at[0], sems.at[index], brow=core_mate).wait_recv()

    order = (4, 3, 5, 2, 6, 1, 7, 0)
    for z in (1, 0):
        for d in order:
            k = z * NY + d
            go(
                remote(
                    pcol.at[row_id((zl + z) % 2, (y + d) % NY, 1 - core)],
                    near_buf.at[k], near_send.at[k], near_recv.at[k], brow=core_mate,
                )
            )
    for d in (2, 1, 3, 0):
        for m, e in enumerate((2, 1, 3)):
            go(
                remote(
                    prow.at[((zh + d) % NZH) * NX + (x + e) % NX],
                    side_buf.at[3 * d + e - 1], side_send.at[3 * d + m], side_recv.at[3 * d + e - 1],
                    bcol=zh * NX + (x + e) % NX,
                )
            )
    for d in order:
        k = NY + d
        arrived(near_buf, near_recv, k)
        near_sum[k] = near_buf[k] + pcol[row_id(1 - zl, (y + d) % NY, core)]
        go(remote(near_sum.at[k], pass_buf.at[d], pass_send.at[d], pass_recv.at[d], brow=z_mate))
    for d in (2, 1, 3, 0):
        for e in (1, 3, 2):
            arrived(side_buf, side_recv, 3 * d + e - 1)
        total = prow[((zh + d) % NZH) * NX + x]
        for e in (1, 3, 2):
            total = total + side_buf[3 * d + e - 1]
        side_sum[d] = total
        if d:
            go(
                remote(
                    side_sum.at[d], hi_buf.at[d - 1], hi_send.at[d - 1], hi_recv.at[d - 1],
                    bcol=((zh + d) % NZH) * NX + x,
                )
            )
    for d in order:
        arrived(near_buf, near_recv, d)
        near_sum[d] = near_buf[d] + pcol[row_id(zl, (y + d) % NY, core)]
        arrived(pass_buf, pass_recv, d)
        pass_sum[d] = near_sum[d] + pass_buf[d]
        if d:
            go(
                remote(
                    pass_sum.at[d], far_buf.at[d - 1], far_send.at[d - 1], far_recv.at[d - 1],
                    brow=row_id(zl, (y + d) % NY, core),
                )
            )
    total = side_sum[0] + pass_sum[0]
    for d in (1, 3, 2):
        arrived(hi_buf, hi_recv, d - 1)
        total = total + hi_buf[d - 1]
    for d in (1, 7, 2, 6, 3, 5, 4):
        arrived(far_buf, far_recv, d - 1)
        total = total + far_buf[d - 1]
    out[...] = total
    for copy in sent:
        copy.wait_send()


def scatter(prow, pcol):
    vmem = pl.BlockSpec(memory_space=pltpu.VMEM)
    dma = pltpu.SemaphoreType.DMA

    def pieces(n):
        return pltpu.VMEM((n, VECS, PIECE), jnp.float32)

    return pl.pallas_call(
        scatter_kernel,
        name="scatter",
        in_specs=[vmem, vmem],
        out_specs=vmem,
        out_shape=jax.ShapeDtypeStruct((VECS, PIECE), jnp.float32),
        scratch_shapes=[pieces(16), pieces(16), pieces(8), pieces(8), pieces(7), pieces(12), pieces(4), pieces(3)]
        + [dma((n,)) for n in (16, 16, 8, 8, 7, 7, 12, 12, 3, 3)],
        compiler_params=pltpu.CompilerParams(collective_id=1, has_side_effects=True),
    )(prow, pcol)


def body(vectors, tiles, tile_rows, tile_cols, counts):
    tt = prep(tiles)
    col, row = gather(vectors)
    prow, pcol = apply(tile_rows, tile_cols, counts, tt, col, row)
    return scatter(prow, pcol)


def solution(mesh):
    return jax.shard_map(
        body,
        mesh=mesh,
        in_specs=(
            P(None, ("brow", "bcol")),
            P(("brow", "bcol"), None),
            P(("brow", "bcol")),
            P(("brow", "bcol")),
            P("brow", "bcol"),
        ),
        out_specs=P(None, ("brow", "bcol")),
        check_vma=False,
    )
```

time: 324 us -> 89.5 us (0.28)
  the two profiles are of different devices: /device:TPU:6 before, /device:TPU:1 now
where the time goes in v1:
time: 89.5 us; the launch traced here: 88.4 us
  Pallas kernels  86.3 us (96%)
  local copies, waits for them, and re-layouts  1.47 us (2%)
    pallas_call x1, Pallas kernels, scatter(): pl.pallas_call(scatter_kernel, name='scatter', in_specs=[vmem, vmem], out...  38.4 us
    pallas_call x1, Pallas kernels, gather(): pl.pallas_call(gather_kernel, name='gather', in_specs=[vmem], out_specs=[...  30.3 us
    pallas_call x1, Pallas kernels, apply(): pl.pallas_call(apply_kernel, name='apply', in_specs=[smem, smem, smem, vm...  9.06 us
    pallas_call x1, Pallas kernels, prep(): pl.pallas_call(prep_kernel, name='prep', grid=(SLOTS // GROUP,), in_specs...  8.58 us

profile of v1, /device:TPU:1, one launch (start us, length us, event | category | flops | bytes accessed | tf_op | source)
XLA Modules:
  0.0 88.4 jit_solution(7523083250556734904)
XLA Ops:
  0.7 30.3 %gather.1 = (bf16[32,8,2048]{2,1,0:T(8,128)(2,1)}, bf16[16,8,2048]{2,1,0:T(8,128)(2,1)}) custom-call(bf16[8,2048]{1,0:T(8,128)(2,1)} %vec.1), custom_call_target="tpu_custom_call" | custom-call | tf_op jit(solution)/shard_map/gather/pallas_call | solution.py:164
  31.0 8.6 %prep.1.tt = bf16[192,64,128]{2,1,0:T(8,128)(2,1)} custom-call(bf16[192,4096]{1,0:T(8,128)(2,1)} %tiles_ref.1), custom_call_target="tpu_custom_call" | custom-call | tf_op jit(solution)/shard_map/prep/pallas_call | solution.py:67
  39.5 9.1 %apply.1 = (f32[16,8,2048]{2,1,0:T(8,128)}, f32[32,8,2048]{2,1,0:T(8,128)}) custom-call(s32[192]{0:T(256)} %rows.1, s32[192]{0:T(256)} %cols.1, s32[1,1]{1,0:T(1,128)S(6)} %copy.7.counts, bf16[192,64,128]{2,1,0:T(8,128)(2,1)} %prep.1.tt, bf16[32,8,2048]{2,1,0:T(8,128)(2,1)} %get-tuple-element.9.col, bf16[16,8,2048]{2,1,0:T(8,128)(2,1)} %get-tuple-element.10.row), custom_call_target="tpu_custom_call" | custom-call | tf_op jit(solution)/shard_map/apply/pallas_call | solution.py:216
  48.6 38.4 %scatter.1 = f32[8,2048]{1,0:T(8,128)} custom-call(f32[16,8,2048]{2,1,0:T(8,128)} %get-tuple-element.11.prow, f32[32,8,2048]{2,1,0:T(8,128)} %get-tuple-element.12.pcol), custom_call_target="tpu_custom_call" | custom-call | tf_op jit(solution)/shard_map/scatter/pallas_call | solution.py:314
  87.0 1.5 %copy.8 = f32[8,2048]{1,0:T(8,128)} copy(f32[8,2048]{1,0:T(8,128)} %scatter.1) | data formatting | bytes 131072

commit v2 on v1

--- a/solution.py
+++ b/solution.py
@@ -15,6 +15,9 @@
 NY, NX, NZH = 8, 4, 4
 ROWS, COLS = 32, 16
 GROUP = 16
+WIRE = PIECE + 128
+FULL = 32000.0
+VMEM = 16 << 20
 
 
 def place():
@@ -47,43 +50,52 @@
         call(bcol=zh * NX + (x + d) % NX)
     call(brow=row_id(1 - zl, y, core))
     call(brow=row_id(zl, y, 1 - core))
-    pl.semaphore_wait(barrier, 15)
-
-
-def prep_kernel(tiles_ref, out_ref, flat, woven):
+
+
+def meet():
+    pl.semaphore_wait(pltpu.get_barrier_semaphore(), 15)
+
+
+def prep_group(g, tiles, out, flat, woven):
     lane = lax.broadcasted_iota(jnp.int32, (32, 128), 1)
+    slots = pl.ds(pl.multiple_of(g * GROUP, GROUP), GROUP)
     for b in range(32):
-        flat[b * GROUP : (b + 1) * GROUP, :] = tiles_ref[:, b * 128 : (b + 1) * 128].astype(jnp.float32)
+        flat[b * GROUP : (b + 1) * GROUP, :] = tiles[slots, b * 128 : (b + 1) * 128].astype(jnp.float32)
     for s in range(GROUP):
         m = flat[pl.ds(s, 32, stride=GROUP), :]
         turned = pltpu.roll(m, 64, 1)
         woven[pl.ds(s * TILE, 32, stride=2), :] = jnp.where(lane < 64, m, turned)
         woven[pl.ds(s * TILE + 1, 32, stride=2), :] = jnp.where(lane < 64, turned, m)
     for s in range(GROUP):
-        out_ref[s] = woven[s * TILE : (s + 1) * TILE, :].astype(jnp.bfloat16)
-
-
-def prep(tiles):
-    return pl.pallas_call(
-        prep_kernel,
-        name="prep",
-        grid=(SLOTS // GROUP,),
-        in_specs=[pl.BlockSpec((GROUP, TILE * TILE), lambda g: (g, 0))],
-        out_specs=pl.BlockSpec((GROUP, TILE, 128), lambda g: (g, 0, 0)),
-        out_shape=jax.ShapeDtypeStruct((SLOTS, TILE, 128), jnp.bfloat16),
-        scratch_shapes=[
-            pltpu.VMEM((32 * GROUP, 128), jnp.float32),
-            pltpu.VMEM((TILE * GROUP, 128), jnp.float32),
-        ],
-    )(tiles)
-
-
-def gather_kernel(vec, col, row, col_send, col_recv, pass_send, near_send, row_send, row_recv, side_send, own_sem):
+        out[g * GROUP + s] = woven[s * TILE : (s + 1) * TILE, :].astype(jnp.bfloat16)
+
+
+def gather_kernel(
+    vec, tiles_hbm, col, row, tt, tiles, flat, woven,
+    col_send, col_recv, pass_send, near_send, row_send, row_recv, side_send, own_sem, tile_sem,
+):
     r, c, zl, y, core, zh, x = place()
     z_mate = row_id(1 - zl, y, core)
     core_mate = row_id(zl, y, 1 - core)
+    halves = [
+        pltpu.make_async_copy(tiles_hbm.at[pl.ds(h * 48, 48)], tiles.at[pl.ds(h * 48, 48)], tile_sem.at[h])
+        for h in range(4)
+    ]
+    for copy in halves:
+        copy.start()
     greet(r, c, zl, y, core, zh, x)
     sent = []
+
+    def prep(lo, hi):
+        def one(g, carry):
+            prep_group(g, tiles, tt, flat, woven)
+            return carry
+
+        lax.fori_loop(lo, hi, one, 0)
+
+    halves[0].wait()
+    prep(0, 3)
+    meet()
 
     def go(copy):
         copy.start()
@@ -106,6 +118,8 @@
     ]
     for copy in mine:
         copy.start()
+    halves[1].wait()
+    prep(3, 5)
 
     def forward_y(n, d):
         src = row_id(zl, (y + d) % NY, core)
@@ -132,20 +146,28 @@
     forward_y(2, 7)
     forward_zh(1, 1)
     forward_zh(2, 3)
+    prep(5, 6)
     forward_y(3, 2)
     forward_y(4, 6)
     forward_z(8, 0)
     forward_zh(3, 2)
+    halves[2].wait()
+    prep(6, 7)
     forward_y(5, 3)
     forward_y(6, 5)
     forward_z(9, 1)
     forward_z(10, 7)
     forward_y(7, 4)
+    prep(7, 9)
     forward_z(11, 2)
     forward_z(12, 6)
+    halves[3].wait()
+    prep(9, 10)
     forward_z(13, 3)
     forward_z(14, 5)
+    prep(10, 11)
     forward_z(15, 4)
+    prep(11, 12)
     for copy in mine:
         copy.wait()
     for z in (0, 1):
@@ -158,21 +180,27 @@
         copy.wait_send()
 
 
-def gather(vectors):
+def gather(vectors, tiles):
     vmem = pl.BlockSpec(memory_space=pltpu.VMEM)
     dma = pltpu.SemaphoreType.DMA
     return pl.pallas_call(
         gather_kernel,
         name="gather",
-        in_specs=[vmem],
-        out_specs=[vmem, vmem],
+        in_specs=[vmem, pl.BlockSpec(memory_space=pltpu.HBM)],
+        out_specs=[vmem, vmem, vmem],
         out_shape=[
             jax.ShapeDtypeStruct((ROWS, VECS, PIECE), jnp.bfloat16),
             jax.ShapeDtypeStruct((COLS, VECS, PIECE), jnp.bfloat16),
+            jax.ShapeDtypeStruct((SLOTS, TILE, 128), jnp.bfloat16),
         ],
-        scratch_shapes=[dma((7,)), dma((ROWS,)), dma((8,)), dma((16,)), dma((3,)), dma((COLS,)), dma((12,)), dma((3,))],
-        compiler_params=pltpu.CompilerParams(collective_id=0, has_side_effects=True),
-    )(vectors)
+        scratch_shapes=[
+            pltpu.VMEM((SLOTS, TILE * TILE), jnp.bfloat16),
+            pltpu.VMEM((32 * GROUP, 128), jnp.float32),
+            pltpu.VMEM((TILE * GROUP, 128), jnp.float32),
+        ]
+        + [dma((n,)) for n in (7, ROWS, 8, 16, 3, COLS, 12, 3, 4)],
+        compiler_params=pltpu.CompilerParams(collective_id=0, has_side_effects=True, vmem_limit_bytes=VMEM),
+    )(vectors, tiles)
 
 
 def apply_kernel(rows, cols, counts, tt, col, row, prow, pcol):
@@ -222,11 +250,41 @@
             jax.ShapeDtypeStruct((COLS, VECS, PIECE), jnp.float32),
             jax.ShapeDtypeStruct((ROWS, VECS, PIECE), jnp.float32),
         ],
+        compiler_params=pltpu.CompilerParams(vmem_limit_bytes=VMEM),
     )(tile_rows, tile_cols, counts, tt, col, row)
 
 
+def blocks():
+    return [slice(q * 128, (q + 1) * 128) for q in range(PIECE // 128)]
+
+
+def pack(parts, wire):
+    top = functools.reduce(jnp.maximum, [jnp.abs(p) for p in parts])
+    power = jnp.floor(jnp.log2(jnp.maximum(top, 1e-30))) + 1.0
+    scale = jnp.exp2(-power) * FULL
+    for cut, p in zip(blocks(), parts):
+        wire[:, cut] = jnp.round(p * scale).astype(jnp.int32).astype(jnp.int16)
+    wire[:, PIECE:] = power.astype(jnp.int32).astype(jnp.int16)
+
+
+def unpack(wire):
+    def wide(cut):
+        return wire[:, cut].astype(jnp.int32).astype(jnp.float32)
+
+    scale = jnp.exp2(wide(slice(PIECE, WIRE))) * (1.0 / FULL)
+    return [wide(cut) * scale for cut in blocks()]
+
+
+def split(ref):
+    return [ref[:, cut] for cut in blocks()]
+
+
+def add(a, b):
+    return [p + q for p, q in zip(a, b)]
+
+
 def scatter_kernel(
-    prow, pcol, out, near_buf, near_sum, pass_buf, pass_sum, far_buf, side_buf, side_sum, hi_buf,
+    prow, pcol, out, near_buf, pass_out, pass_buf, far_out, far_buf, side_out, side_buf, hi_out, hi_buf,
     near_send, near_recv, pass_send, pass_recv, far_send, far_recv, side_send, side_recv, hi_send, hi_recv,
 ):
     r, c, zl, y, core, zh, x = place()
@@ -242,6 +300,17 @@
     def arrived(buf, sems, index):
         remote(buf.at[index], buf.at[index], near_send.at[0], sems.at[index], brow=core_mate).wait_recv()
 
+    def side_pack(d, e):
+        k = 3 * d + e - 1
+        pack(split(prow.at[((zh + d) % NZH) * NX + (x + e) % NX]), side_out.at[k])
+
+    def side_go(d, e):
+        k = 3 * d + e - 1
+        go(remote(side_out.at[k], side_buf.at[k], side_send.at[k], side_recv.at[k], bcol=zh * NX + (x + e) % NX))
+
+    for e in (2, 1, 3):
+        side_pack(2, e)
+    meet()
     order = (4, 3, 5, 2, 6, 1, 7, 0)
     for z in (1, 0):
         for d in order:
@@ -252,54 +321,79 @@
                     near_buf.at[k], near_send.at[k], near_recv.at[k], brow=core_mate,
                 )
             )
-    for d in (2, 1, 3, 0):
-        for m, e in enumerate((2, 1, 3)):
-            go(
-                remote(
-                    prow.at[((zh + d) % NZH) * NX + (x + e) % NX],
-                    side_buf.at[3 * d + e - 1], side_send.at[3 * d + m], side_recv.at[3 * d + e - 1],
-                    bcol=zh * NX + (x + e) % NX,
-                )
-            )
-    for d in order:
+    for e in (2, 1, 3):
+        side_go(2, e)
+
+    def pass_on(d):
         k = NY + d
         arrived(near_buf, near_recv, k)
-        near_sum[k] = near_buf[k] + pcol[row_id(1 - zl, (y + d) % NY, core)]
-        go(remote(near_sum.at[k], pass_buf.at[d], pass_send.at[d], pass_recv.at[d], brow=z_mate))
-    for d in (2, 1, 3, 0):
+        pack(add(split(near_buf.at[k]), split(pcol.at[row_id(1 - zl, (y + d) % NY, core)])), pass_out.at[d])
+        go(remote(pass_out.at[d], pass_buf.at[d], pass_send.at[d], pass_recv.at[d], brow=z_mate))
+
+    def side_on(d):
+        for e in (2, 1, 3):
+            side_pack(d, e)
+            side_go(d, e)
+
+    def side_sum(d):
+        total = split(prow.at[((zh + d) % NZH) * NX + x])
         for e in (1, 3, 2):
             arrived(side_buf, side_recv, 3 * d + e - 1)
-        total = prow[((zh + d) % NZH) * NX + x]
-        for e in (1, 3, 2):
-            total = total + side_buf[3 * d + e - 1]
-        side_sum[d] = total
-        if d:
-            go(
-                remote(
-                    side_sum.at[d], hi_buf.at[d - 1], hi_send.at[d - 1], hi_recv.at[d - 1],
-                    bcol=((zh + d) % NZH) * NX + x,
-                )
-            )
-    for d in order:
+            total = add(total, unpack(side_buf.at[3 * d + e - 1]))
+        return total
+
+    def hi_on(d):
+        pack(side_sum(d), hi_out.at[d - 1])
+        go(
+            remote(
+                hi_out.at[d - 1], hi_buf.at[d - 1], hi_send.at[d - 1], hi_recv.at[d - 1],
+                bcol=((zh + d) % NZH) * NX + x,
+            )
+        )
+
+    def far_sum(d):
         arrived(near_buf, near_recv, d)
-        near_sum[d] = near_buf[d] + pcol[row_id(zl, (y + d) % NY, core)]
+        total = add(split(near_buf.at[d]), split(pcol.at[row_id(zl, (y + d) % NY, core)]))
         arrived(pass_buf, pass_recv, d)
-        pass_sum[d] = near_sum[d] + pass_buf[d]
-        if d:
-            go(
-                remote(
-                    pass_sum.at[d], far_buf.at[d - 1], far_send.at[d - 1], far_recv.at[d - 1],
-                    brow=row_id(zl, (y + d) % NY, core),
-                )
-            )
-    total = side_sum[0] + pass_sum[0]
+        return add(total, unpack(pass_buf.at[d]))
+
+    def far_on(d):
+        pack(far_sum(d), far_out.at[d - 1])
+        go(
+            remote(
+                far_out.at[d - 1], far_buf.at[d - 1], far_send.at[d - 1], far_recv.at[d - 1],
+                brow=row_id(zl, (y + d) % NY, core),
+            )
+        )
+
+    pass_on(4)
+    side_on(1)
+    pass_on(3)
+    pass_on(5)
+    side_on(3)
+    pass_on(2)
+    pass_on(6)
+    side_on(0)
+    far_on(4)
+    hi_on(2)
+    pass_on(1)
+    pass_on(7)
+    far_on(3)
+    hi_on(1)
+    pass_on(0)
+    far_on(5)
+    hi_on(3)
+    for d in (2, 6, 1, 7):
+        far_on(d)
+    total = add(side_sum(0), far_sum(0))
     for d in (1, 3, 2):
         arrived(hi_buf, hi_recv, d - 1)
-        total = total + hi_buf[d - 1]
+        total = add(total, unpack(hi_buf.at[d - 1]))
     for d in (1, 7, 2, 6, 3, 5, 4):
         arrived(far_buf, far_recv, d - 1)
-        total = total + far_buf[d - 1]
-    out[...] = total
+        total = add(total, unpack(far_buf.at[d - 1]))
+    for cut, p in zip(blocks(), total):
+        out[:, cut] = p
     for copy in sent:
         copy.wait_send()
 
@@ -308,8 +402,8 @@
     vmem = pl.BlockSpec(memory_space=pltpu.VMEM)
     dma = pltpu.SemaphoreType.DMA
 
-    def pieces(n):
-        return pltpu.VMEM((n, VECS, PIECE), jnp.float32)
+    def wires(n):
+        return pltpu.VMEM((n, VECS, WIRE), jnp.int16)
 
     return pl.pallas_call(
         scatter_kernel,
@@ -317,15 +411,18 @@
         in_specs=[vmem, vmem],
         out_specs=vmem,
         out_shape=jax.ShapeDtypeStruct((VECS, PIECE), jnp.float32),
-        scratch_shapes=[pieces(16), pieces(16), pieces(8), pieces(8), pieces(7), pieces(12), pieces(4), pieces(3)]
+        scratch_shapes=[pltpu.VMEM((16, VECS, PIECE), jnp.float32)]
+        + [wires(n) for n in (8, 8, 7, 7, 12, 12, 3, 3)]
         + [dma((n,)) for n in (16, 16, 8, 8, 7, 7, 12, 12, 3, 3)],
-        compiler_params=pltpu.CompilerParams(collective_id=1, has_side_effects=True),
+        compiler_params=pltpu.CompilerParams(collective_id=1, has_side_effects=True, vmem_limit_bytes=VMEM),
     )(prow, pcol)
 
 
 def body(vectors, tiles, tile_rows, tile_cols, counts):
-    tt = prep(tiles)
-    col, row = gather(vectors)
+    tiles, tile_rows, tile_cols = (
+        pltpu.with_memory_space_constraint(a, pltpu.HBM) for a in (tiles, tile_rows, tile_cols)
+    )
+    col, row, tt = gather(vectors, tiles)
     prow, pcol = apply(tile_rows, tile_cols, counts, tt, col, row)
     return scatter(prow, pcol)
 

time: 89.5 us -> 58.5 us (0.65)
  the two profiles are of different devices: /device:TPU:1 before, /device:TPU:6 now
where the time goes in v2:
time: 58.5 us; the launch traced here: 57.8 us
  Pallas kernels  55.7 us (95%)
  local copies, waits for them, and re-layouts  1.38 us (2%)
  between operations  0.68 us (1%)
    pallas_call x1, Pallas kernels, gather(): pl.pallas_call(gather_kernel, name='gather', in_specs=[vmem, pl.BlockSpec...  27.1 us
    pallas_call x1, Pallas kernels, scatter(): pl.pallas_call(scatter_kernel, name='scatter', in_specs=[vmem, vmem], out...  22.5 us
    pallas_call x1, Pallas kernels, apply(): pl.pallas_call(apply_kernel, name='apply', in_specs=[smem, smem, smem, vm...  6.08 us
    unnamed x3, local copies, waits for them, and re-layouts  1.38 us

profile of v2, /device:TPU:6, one launch (start us, length us, event | category | flops | bytes accessed | tf_op | source)
XLA Modules:
  0.0 57.8 jit_solution(12195951429870187400)
XLA Ops:
  0.7 0.0 copy-start
  0.7 0.7 %copy-done = bf16[8,2048]{1,0:T(8,128)(2,1)S(1)} copy-done((bf16[8,2048]{1,0:T(8,128)(2,1)S(1)}, bf16[8,2048]{1,0:T(8,128)(2,1)}, u32[]{:S(2)}) %copy-start) | copy-done | bytes 32792
  1.4 27.1 %gather.1 = (bf16[32,8,2048]{2,1,0:T(8,128)(2,1)S(1)}, bf16[16,8,2048]{2,1,0:T(8,128)(2,1)S(1)}, bf16[192,64,128]{2,1,0:T(8,128)(2,1)S(1)}) custom-call(bf16[8,2048]{1,0:T(8,128)(2,1)S(1)} %copy-done, bf16[192,4096]{1,0:T(8,128)(2,1)} %tiles_hbm.1), custom_call_target="tpu_custom_call" | custom-call | tf_op jit(solution)/shard_map/gather/pallas_call | solution.py:186
  28.6 6.1 %apply.1 = (f32[16,8,2048]{2,1,0:T(8,128)S(1)}, f32[32,8,2048]{2,1,0:T(8,128)S(1)}) custom-call(s32[192]{0:T(256)} %rows.1, s32[192]{0:T(256)} %cols.1, s32[1,1]{1,0:T(1,128)S(6)} %copy.7.counts, bf16[192,64,128]{2,1,0:T(8,128)(2,1)S(1)} %get-tuple-element.10.tt, bf16[32,8,2048]{2,1,0:T(8,128)(2,1)S(1)} %get-tuple-element.11.col, ...), custom_call_target="tpu_custom_call" | custom-call | tf_op jit(solution)/shard_map/apply/pallas_call | solution.py:244
  34.6 22.5 %scatter.1 = f32[8,2048]{1,0:T(8,128)S(1)} custom-call(f32[16,8,2048]{2,1,0:T(8,128)S(1)} %get-tuple-element.13.prow, f32[32,8,2048]{2,1,0:T(8,128)S(1)} %get-tuple-element.14.pcol), custom_call_target="tpu_custom_call" | custom-call | tf_op jit(solution)/shard_map/scatter/pallas_call | solution.py:408
  57.2 0.6 %copy.8 = f32[8,2048]{1,0:T(8,128)} copy(f32[8,2048]{1,0:T(8,128)S(1)} %scatter.1) | data formatting | bytes 131072
Async XLA Ops:
  0.7 0.8 %copy-start = (bf16[8,2048]{1,0:T(8,128)(2,1)S(1)}, bf16[8,2048]{1,0:T(8,128)(2,1)}, u32[]{:S(2)}) copy-start(bf16[8,2048]{1,0:T(8,128)(2,1)} %vec.1) | copy-start | bytes 98308

commit v3 on v0

v3 whole, which is shorter than its diff:
```python
import functools

import jax
import jax.numpy as jnp
from jax import lax
from jax.experimental import pallas as pl
from jax.experimental.pallas import tpu as pltpu
from jax.sharding import PartitionSpec as P

MESH = pl.DeviceIdType.MESH
TILE = 64
PIECE = 2048
SLOTS = 192
VECS = 8
NY, NX, NZH = 8, 4, 4
ROWS, COLS = 32, 16
GROUP = 16
UNROLL = 32
SPAN = 128
WIRE = PIECE + 128
FULL = 32000.0
VMEM = 32 << 20
BLOCKS = PIECE // 128


def place():
    r = lax.axis_index("brow")
    c = lax.axis_index("bcol")
    return r, c, r // 16, (r // 2) % NY, r % 2, c // NX, c % NX


def row_id(zl, y, core):
    return zl * 16 + y * 2 + core


def remote(src, dst, send, recv, **where):
    return pltpu.make_async_remote_copy(
        src_ref=src, dst_ref=dst, send_sem=send, recv_sem=recv, device_id=where, device_id_type=MESH
    )


def greet(zl, y, core, zh, x):
    barrier = pltpu.get_barrier_semaphore()

    def call(**where):
        pl.semaphore_signal(barrier, inc=1, device_id=where, device_id_type=MESH)

    for d in (2, 6, 1, 7):
        call(brow=row_id(zl, (y + d) % NY, core))
    for d in (2, 1, 3):
        call(bcol=((zh + d) % NZH) * NX + x)
        call(bcol=zh * NX + (x + d) % NX)
    call(brow=row_id(1 - zl, y, core))
    call(brow=row_id(zl, y, 1 - core))


def meet():
    pl.semaphore_wait(pltpu.get_barrier_semaphore(), 12)


def prep_group(g, tiles, out, flat, woven):
    lane = lax.broadcasted_iota(jnp.int32, (32, 128), 1)
    slots = pl.ds(pl.multiple_of(g * GROUP, GROUP), GROUP)
    for b in range(32):
        flat[b * GROUP : (b + 1) * GROUP, :] = tiles[slots, b * 128 : (b + 1) * 128].astype(jnp.float32)
    for s in range(GROUP):
        m = flat[pl.ds(s, 32, stride=GROUP), :]
        turned = pltpu.roll(m, 64, 1)
        woven[pl.ds(s * TILE, 32, stride=2), :] = jnp.where(lane < 64, m, turned)
        woven[pl.ds(s * TILE + 1, 32, stride=2), :] = jnp.where(lane < 64, turned, m)
    for s in range(GROUP):
        out[g * GROUP + s] = woven[s * TILE : (s + 1) * TILE, :].astype(jnp.bfloat16)


def blocks():
    return [slice(q * 128, (q + 1) * 128) for q in range(PIECE // 128)]


def pack(parts, wire):
    top = functools.reduce(jnp.maximum, [jnp.abs(p) for p in parts])
    power = jnp.floor(jnp.log2(jnp.maximum(top, 1e-30))) + 1.0
    scale = jnp.exp2(-power) * FULL
    for cut, p in zip(blocks(), parts):
        wire[:, cut] = jnp.round(p * scale).astype(jnp.int32).astype(jnp.int16)
    wire[:, PIECE:] = power.astype(jnp.int32).astype(jnp.int16)


def unpack(wire):
    def wide(cut):
        return wire[:, cut].astype(jnp.int32).astype(jnp.float32)

    scale = jnp.exp2(wide(slice(PIECE, WIRE))) * (1.0 / FULL)
    return [wide(cut) * scale for cut in blocks()]


def add(a, b):
    return [p + q for p, q in zip(a, b)]


def part(buf, piece):
    return buf.at[pl.ds(pl.multiple_of(piece * BLOCKS * VECS, BLOCKS * VECS), BLOCKS * VECS)]


def split(ref):
    return [ref[q * VECS : (q + 1) * VECS, :] for q in range(BLOCKS)]


def mark(hot, places):
    ids = places[...] >> 1
    ids = jnp.concatenate([ids, ids], axis=1)
    for block in range(hot.shape[0] // 64):
        spots = lax.broadcasted_iota(jnp.int32, (64, 2 * SLOTS), 0) + block * 64
        hot[block * 64 : (block + 1) * 64, :] = jnp.where(spots == ids, 1.0, 0.0).astype(jnp.bfloat16)


def products(to, at, counts, tt, seg, terms, forward):
    n = counts[0, 0]
    high = (lax.broadcasted_iota(jnp.int32, (VECS, 128), 1) >= TILE).astype(jnp.int32)

    def step(g, carry):
        for u in range(UNROLL):
            s = g * UNROLL + u
            dead = ((s >= n).astype(jnp.int32)) * 2
            given, wanted = at[s], to[s]
            own = jnp.where(high == (given & 1) + dead, seg[given >> 1].astype(jnp.float32), 0.0)
            if forward:
                half = lax.dot_general(
                    own.astype(jnp.bfloat16), tt[s], (((1,), (1,)), ((), ())), preferred_element_type=jnp.float32
                )
                both = jnp.concatenate([half, half], axis=1)
            else:
                own = (own + pltpu.roll(own, TILE, 1))[:, :TILE]
                both = jnp.dot(own.astype(jnp.bfloat16), tt[s], preferred_element_type=jnp.float32)
            terms[pl.ds(pl.multiple_of(s * VECS, VECS), VECS), :] = jnp.where(high == (wanted & 1), both, 0.0)
        return carry

    lax.fori_loop(0, SLOTS // UNROLL, step, 0)


def spread(terms, twins, hot, sums):
    for k in range(VECS):
        exact = terms[pl.ds(k, SLOTS, stride=VECS), :]
        top = exact.astype(jnp.bfloat16)
        twins[:SLOTS, k * 128 : (k + 1) * 128] = top
        twins[SLOTS:, k * 128 : (k + 1) * 128] = (exact - top.astype(jnp.float32)).astype(jnp.bfloat16)

    def step(block, carry):
        picks = hot[pl.ds(pl.multiple_of(block * SPAN, SPAN), SPAN), :]
        for k in range(0, VECS, 2):
            total = jnp.dot(picks, twins[:, k * 128 : (k + 2) * 128], preferred_element_type=jnp.float32)
            for m in (0, 1):
                sums[pl.ds(block * SPAN * VECS + k + m, SPAN, stride=VECS), :] = total[:, m * 128 : (m + 1) * 128]
        return carry

    lax.fori_loop(0, hot.shape[0] // SPAN, step, 0)


def kernel(
    cols, rows, counts, cols_vec, rows_vec, vec_hbm, tiles_hbm, out,
    vec, col, row, tiles, tt, flat, woven, pair_hot, side_hot, terms, twins, pcol, prow,
    near_buf, tree_out, tree_buf, more_out, more_buf, side_out, side_buf,
    near_send, tree_send, pass_send, col_recv, row_send, row_recv, own_sem, tile_sem, vec_sem,
    near_out, near_in, tree_from, tree_into, more_from, more_into, side_from, side_into,
):
    r, c, zl, y, core, zh, x = place()
    way = 1 - 2 * core
    halves = [
        pltpu.make_async_copy(tiles_hbm.at[pl.ds(h * 48, 48)], tiles.at[pl.ds(h * 48, 48)], tile_sem.at[h])
        for h in range(4)
    ]
    loads = [
        pltpu.make_async_copy(vec_hbm.at[:, cut], vec.at[q], vec_sem.at[q]) for q, cut in enumerate(blocks())
    ]
    for copy in loads:
        copy.start()
    greet(zl, y, core, zh, x)
    for copy in halves:
        copy.start()

    def prep(lo, hi):
        def one(g, carry):
            prep_group(g, tiles, tt, flat, woven)
            return carry

        lax.fori_loop(lo, hi, one, 0)

    for copy in loads:
        copy.wait()
    meet()

    def ahead(d, plane):
        return row_id(plane, (y + d + NY) % NY, core)

    def across(d, e):
        return ((zh + d + NZH) % NZH) * NX + (x + e + NX) % NX

    def hunk(buf, piece):
        return buf.at[pl.ds(piece * BLOCKS, BLOCKS)]

    def push_col(piece, sem, to, fresh=False):
        remote(vec if fresh else hunk(col, piece), hunk(col, piece), sem, col_recv.at[piece], brow=to).start()

    def push_row(piece, n, to, fresh=False):
        remote(vec if fresh else hunk(row, piece), hunk(row, piece), row_send.at[n], row_recv.at[piece], bcol=to).start()

    def got_col(piece):
        remote(hunk(col, piece), hunk(col, piece), own_sem.at[0], col_recv.at[piece], brow=r).wait_recv()

    def got_row(piece):
        remote(hunk(row, piece), hunk(row, piece), own_sem.at[0], row_recv.at[piece], bcol=c).wait_recv()

    z_mate = row_id(1 - zl, y, core)
    core_mate = row_id(zl, y, 1 - core)
    push_col(r, pass_send.at[0], z_mate, True)
    for n, d in enumerate((2, -2, 1, -1)):
        push_col(r, tree_send.at[n], ahead(d, zl), True)
    for n, d in enumerate((2, 1, -1)):
        push_row(c, n, across(d, 0), True)
    for n, d in enumerate((1, -1)):
        push_row(c, 3 + n, across(0, d), True)
    push_col(r, near_send.at[0], core_mate, True)
    mine = [
        pltpu.make_async_copy(vec, hunk(col, r), own_sem.at[1]),
        pltpu.make_async_copy(vec, hunk(row, c), own_sem.at[2]),
    ]
    for copy in mine:
        copy.start()
    halves[0].wait()
    prep(0, 3)
    halves[1].wait()
    prep(3, 5)
    mark(pair_hot, cols_vec)
    mark(side_hot, rows_vec)

    def near(n, piece):
        push_col(piece, near_send.at[n], core_mate)

    def branch(plane, way, sems, base, first):
        p = ahead(-2 * way, plane)
        got_col(p)
        push_col(p, sems.at[base], ahead(2 * way, plane))
        push_col(p, sems.at[base + 1], ahead(way, plane))
        near(first, p)
        q = ahead(2 * way, plane)
        got_col(q)
        push_col(q, sems.at[base + 2], ahead(-way, plane))
        near(first + 1, q)
        return p, q

    def side(n, d):
        p = across(d, 0)
        got_row(p)
        push_row(p, 3 + 2 * n, across(0, 1))
        push_row(p, 4 + 2 * n, across(0, -1))

    def far_side():
        p = across(2, 0)
        got_row(p)
        push_row(p, 14, across(0, 2))
        push_row(p, 9, across(0, 1))
        push_row(p, 10, across(0, -1))

    def round_side(n, d):
        p = across(d, -way)
        got_row(p)
        push_row(p, 11 + n, across(0, way))

    @pl.when(core == 0)
    def _():
        p, q = branch(zl, way, tree_send, 4, 1)
        push_col(p, pass_send.at[1], z_mate)
        push_col(q, pass_send.at[2], z_mate)
        side(1, -way)
        side(2, way)
        for n, d in ((3, 1), (4, -1)):
            p = ahead(d, zl)
            got_col(p)
            push_col(p, pass_send.at[n], z_mate)
            near(n, p)
        round_side(0, 0)
        halves[2].wait()
        prep(5, 7)
        far_side()
        for n, d in ((5, 3), (6, -3)):
            p = ahead(d, zl)
            got_col(p)
            push_col(p, pass_send.at[n], z_mate)
            near(n, p)
        round_side(1, -way)
        prep(7, 8)
        p = ahead(4, zl)
        got_col(p)
        push_col(p, pass_send.at[7], z_mate)
        near(7, p)
        round_side(2, way)
        prep(8, 9)
        for n, d in enumerate((0, 2, -2)):
            p = ahead(d, 1 - zl)
            got_col(p)
            near(8 + n, p)
        halves[3].wait()
        prep(9, 10)
        for n, d in enumerate((1, -1, 3, -3, 4)):
            p = ahead(d, 1 - zl)
            got_col(p)
            near(11 + n, p)

    @pl.when(core == 1)
    def _():
        p = ahead(0, 1 - zl)
        got_col(p)
        for n, d in enumerate((2, -2, 1, -1)):
            push_col(p, pass_send.at[1 + n], ahead(d, zl))
        near(1, p)
        branch(zl, way, tree_send, 4, 2)
        side(1, -way)
        side(2, way)
        for n, d in ((4, 1), (5, -1)):
            p = ahead(d, zl)
            got_col(p)
            near(n, p)
        round_side(0, 0)
        halves[2].wait()
        prep(5, 7)
        far_side()
        p = ahead(-2, 1 - zl)
        got_col(p)
        push_col(p, pass_send.at[5], ahead(2, zl))
        push_col(p, pass_send.at[6], ahead(1, zl))
        near(6, p)
        q = ahead(2, 1 - zl)
        got_col(q)
        push_col(q, pass_send.at[7], ahead(-1, zl))
        near(7, q)
        round_side(1, -way)
        prep(7, 8)
        for n, d in enumerate((3, -3, 4)):
            p = ahead(d, zl)
            got_col(p)
            near(8 + n, p)
        round_side(2, way)
        prep(8, 9)
        for n, d in enumerate((1, -1)):
            p = ahead(d, 1 - zl)
            got_col(p)
            near(11 + n, p)
        halves[3].wait()
        prep(9, 10)
        for n, d in enumerate((3, -3, 4)):
            p = ahead(d, 1 - zl)
            got_col(p)
            near(13 + n, p)

    prep(10, 12)
    for copy in mine:
        copy.wait()
    for d in range(NZH):
        got_row(across(d, way))
        got_row(across(d, 2))
    got_row(across(2, -way))
    products(cols, rows, counts, tt, row, terms, False)
    spread(terms, twins, pair_hot, pcol)

    def rel(d):
        return (d + NY) % NY

    def near_go(plane, d):
        k = plane * NY + rel(d)
        src = row_id((zl + plane) % 2, (y + d + NY) % NY, 1 - core)
        remote(part(pcol, src), near_buf.at[k], near_out.at[k], near_in.at[k], brow=core_mate).start()

    for d in (4, -3, 3, -2, 2, -1, 1, 0):
        near_go(1, d)
        near_go(0, d)
    for z in (0, 1):
        for d in range(NY):
            got_col(row_id((zl + z) % 2, (y + d) % NY, 1 - core))
    products(rows, cols, counts, tt, col, terms, True)
    spread(terms, twins, side_hot, prow)

    tree = (tree_out, tree_buf, tree_from, tree_into)
    more = (more_out, more_buf, more_from, more_into)
    side_kind = (side_out, side_buf, side_from, side_into)

    def send(kind, n, value, **to):
        held, buf, sends, recvs = kind
        pack(value, held.at[n])
        remote(held.at[n], buf.at[n], sends.at[n], recvs.at[n], **to).start()

    def take(kind, n, value):
        held, buf, _, recvs = kind
        remote(buf.at[n], buf.at[n], own_sem.at[0], recvs.at[n], brow=core_mate).wait_recv()
        return add(value, unpack(buf.at[n]))

    def pair(plane, d):
        k = plane * NY + rel(d)
        remote(near_buf.at[k], near_buf.at[k], own_sem.at[0], near_in.at[k], brow=core_mate).wait_recv()
        other = row_id((zl + plane) % 2, (y + d + NY) % NY, core)
        return add(split(near_buf.at[k]), split(part(pcol, other)))

    def own_row(d, e):
        return split(part(prow, across(d, e)))


    def outer(kind, way, value):
        send(kind, 1, value(-4 * way), brow=ahead(-2 * way, zl))
        send(kind, 0, value(-3 * way), brow=ahead(-way, zl))
        send(kind, 2, value(3 * way), brow=ahead(way, zl))

    def inner(kind, way, value):
        send(kind, 5, value(-way), brow=ahead(-way, zl))
        send(kind, 6, value(way), brow=ahead(way, zl))

    def middle(kind, way, value):
        send(kind, 4, take(kind, 2, value(2 * way)), brow=ahead(2 * way, zl))
        send(kind, 3, take(kind, 1, take(kind, 0, value(-2 * way))), brow=ahead(-2 * way, zl))

    def gathered(kind, value):
        for n in (5, 6, 4, 3):
            value = take(kind, n, value)
        return value

    def row_out_two(n, d):
        send(side_kind, 3 * n, own_row(d, 2), bcol=across(0, -way))
        send(side_kind, 3 * n + 1, own_row(d, way), bcol=across(0, way))

    def row_out_one(n, d):
        send(side_kind, 3 * n + 2, take(side_kind, 3 * n, own_row(d, -way)), bcol=across(0, -way))

    def row_sum(n, d):
        return take(side_kind, 3 * n + 2, take(side_kind, 3 * n + 1, own_row(d, 0)))

    def finish(total):
        for cut, p in zip(blocks(), total):
            out[:, cut] = p

    def row_total(total):
        total = add(total, row_sum(3, 0))
        for n in (13, 14, 12):
            total = take(side_kind, n, total)
        return total

    def row_far():
        send(side_kind, 0, own_row(2, 2), bcol=across(0, 2))
        send(side_kind, 1, own_row(2, way), bcol=across(0, way))
        send(side_kind, 2, own_row(2, -way), bcol=across(0, -way))

    def row_two():
        total = own_row(2, 0)
        for n in (2, 1, 0):
            total = take(side_kind, n, total)
        send(side_kind, 12, total, bcol=across(2, 0))

    def row_plus():
        send(side_kind, 13, row_sum(2, way), bcol=across(way, 0))

    def row_minus():
        send(side_kind, 14, row_sum(1, -way), bcol=across(-way, 0))

    @pl.when(core == 0)
    def _():

        def cross(d):
            send(more, rel(d), pair(1, d), brow=z_mate)

        def value(d):
            return take(more, rel(d), pair(0, d))

        row_out_two(1, -way)
        cross(4)
        cross(-3)
        cross(3)
        row_out_two(2, way)
        cross(-2)
        cross(2)
        row_far()
        cross(-1)
        cross(1)
        row_out_one(1, -way)
        cross(0)
        row_out_two(3, 0)
        outer(tree, way, value)
        row_out_one(2, way)
        row_two()
        row_minus()
        row_plus()
        middle(tree, way, value)
        row_out_one(3, 0)
        inner(tree, way, value)
        finish(row_total(gathered(tree, value(0))))

    @pl.when(core == 1)
    def _():

        def mine(d):
            return pair(0, d)

        def others(d):
            return pair(1, d)

        row_out_two(1, -way)
        outer(more, 1, others)
        row_out_two(2, way)
        outer(tree, way, mine)
        row_far()
        row_out_one(1, -way)
        row_out_two(3, 0)
        row_out_one(2, way)
        middle(more, 1, others)
        inner(more, 1, others)
        row_two()
        row_minus()
        row_plus()
        middle(tree, way, mine)
        inner(tree, way, mine)
        row_out_one(3, 0)
        send(more, 7, gathered(more, others(0)), brow=z_mate)
        finish(take(more, 7, row_total(gathered(tree, mine(0)))))

    for n in range(16):
        remote(part(pcol, 0), near_buf.at[0], near_out.at[n], own_sem.at[0], brow=core_mate).wait_send()
    for (held, buf, sends, recvs), count in ((tree, 7), (more, 8), (side_kind, 15)):
        for n in range(count):
            remote(held.at[n], buf.at[n], sends.at[n], own_sem.at[0], brow=core_mate).wait_send()
    for sems, count in ((near_send, 16), (tree_send, 7), (pass_send, 8)):
        for n in range(count):
            remote(vec, hunk(col, r), sems.at[n], own_sem.at[0], brow=core_mate).wait_send()
    for n in range(15):
        remote(vec, hunk(row, c), row_send.at[n], own_sem.at[0], bcol=c).wait_send()


def body(vectors, tiles, tile_rows, tile_cols, counts):
    vmem = pl.BlockSpec(memory_space=pltpu.VMEM)
    smem = pl.BlockSpec(memory_space=pltpu.SMEM)
    hbm = pl.BlockSpec(memory_space=pltpu.HBM)
    dma = pltpu.SemaphoreType.DMA
    bf16, f32 = jnp.bfloat16, jnp.float32

    def wires(n):
        return [pltpu.VMEM((n, VECS, WIRE), jnp.int16)] * 2

    def far(a):
        return pltpu.with_memory_space_constraint(a, pltpu.HBM)

    return pl.pallas_call(
        kernel,
        name="block_sparse",
        in_specs=[smem, smem, smem, vmem, vmem, hbm, hbm],
        out_specs=vmem,
        out_shape=jax.ShapeDtypeStruct((VECS, PIECE), f32),
        scratch_shapes=[
            pltpu.VMEM((BLOCKS, VECS, 128), bf16),
            pltpu.VMEM((ROWS * BLOCKS, VECS, 128), bf16),
            pltpu.VMEM((COLS * BLOCKS, VECS, 128), bf16),
            pltpu.VMEM((SLOTS, TILE * TILE), bf16),
            pltpu.VMEM((SLOTS, TILE, 128), bf16),
            pltpu.VMEM((32 * GROUP, 128), f32),
            pltpu.VMEM((TILE * GROUP, 128), f32),
            pltpu.VMEM((ROWS * BLOCKS, 2 * SLOTS), bf16),
            pltpu.VMEM((COLS * BLOCKS, 2 * SLOTS), bf16),
            pltpu.VMEM((SLOTS * VECS, 128), f32),
            pltpu.VMEM((2 * SLOTS, VECS * 128), bf16),
            pltpu.VMEM((ROWS * BLOCKS * VECS, 128), f32),
            pltpu.VMEM((COLS * BLOCKS * VECS, 128), f32),
            pltpu.VMEM((16, BLOCKS * VECS, 128), f32),
            *wires(7), *wires(8), *wires(15),
        ]
        + [dma((n,)) for n in (16, 7, 8, ROWS, 15, COLS, 3, 4, BLOCKS)]
        + [dma((n,)) for n in (16, 16, 7, 7, 8, 8, 15, 15)],
        compiler_params=pltpu.CompilerParams(collective_id=0, has_side_effects=True, vmem_limit_bytes=VMEM),
    )(
        far(tile_cols), far(tile_rows), counts, tile_cols.reshape(1, SLOTS), tile_rows.reshape(1, SLOTS),
        far(vectors), far(tiles),
    )


def solution(mesh):
    return jax.shard_map(
        body,
        mesh=mesh,
        in_specs=(
            P(None, ("brow", "bcol")),
            P(("brow", "bcol"), None),
            P(("brow", "bcol")),
            P(("brow", "bcol")),
            P("brow", "bcol"),
        ),
        out_specs=P(None, ("brow", "bcol")),
        check_vma=False,
    )
```

time: 324 us -> 49.7 us (0.15)
  waiting for transfers between devices: 224 us -> 0 us
  Pallas kernels: 0 us -> 47.7 us
  blocking collectives: 40.4 us -> 0 us
  local copies, waits for them, and re-layouts: 31.9 us -> 0.63 us
  between operations: 13.8 us -> 0.66 us
  matrix products: 11.4 us -> 0 us
    reduce_scatter x2 -> x0, waiting for transfers between devices: 159 us -> none  [the longest x1 123 us: body(): lax.psum_scatter(partial_cols, 'brow', scatter_dimension=1, tiled=True)]
    all_gather x1 -> x0, waiting for transfers between devices: 64.3 us -> none  [body(): lax.all_gather(vectors, 'brow', axis=1, tiled=True)]
    pallas_call x0 -> x1, Pallas kernels: none -> 47.7 us  [body(): pl.pallas_call(kernel, name='block_sparse', in_specs=[smem, smem, smem, v...]
    all_gather x1 -> x0, blocking collectives: 40.4 us -> none  [body(): lax.all_gather(vectors, 'bcol', axis=1, tiled=True)]
    reshape x5 -> x0, local copies, waits for them, and re-layouts: 19.7 us -> none  [the longest x1 4.75 us: body(): partial_cols = partial_cols.reshape(width, col_tiles * side)]
    dot_general x6 -> x0, matrix products: 11.4 us -> none  [the longest x1 3.15 us: body(): jnp.einsum('tc,kcj->tkj', col_hot, col_seg, preferred_element_type=jnp.fl...]
    transpose x2 -> x0, local copies, waits for them, and re-layouts: 5.9 us -> none  [the longest x1 3.19 us: body(): jnp.einsum('tr,tki->kri', row_hot_wide, forward, precision=lax.Precision....]
    unnamed x7 -> x1, local copies, waits for them, and re-layouts: 3.87 us -> 0.63 us
  transfers between devices with their start and end apart: 3 -> 0, of which waited for: 3 -> 0; matrix products, arithmetic and copies ran while one was open for 8% -> 0% of each run, Pallas kernels for 0% -> 0%
where the time goes in v3:
time: 49.7 us; the launch traced here: 49 us
  Pallas kernels  47.7 us (96%)
  between operations  0.66 us (1%)
  local copies, waits for them, and re-layouts  0.63 us (1%)
    pallas_call x1, Pallas kernels, body(): pl.pallas_call(kernel, name='block_sparse', in_specs=[smem, smem, smem, v...  47.7 us

profile of v3, /device:TPU:6, one launch (start us, length us, event | category | flops | bytes accessed | tf_op | source)
XLA Modules:
  0.0 49.0 jit_solution(12112107277164737197)
XLA Ops:
  0.7 47.7 %block_sparse.1 = f32[8,2048]{1,0:T(8,128)S(1)} custom-call(s32[192]{0:T(256)} %cols.1, s32[192]{0:T(256)} %rows.1, s32[1,1]{1,0:T(1,128)S(6)} %copy.7.counts, s32[1,192]{1,0:T(1,128)} %bitcast.2, s32[1,192]{1,0:T(1,128)} %bitcast.3, bf16[8,2048]{1,0:T(8,128)(2,1)} %vec_hbm.1, bf16[192,4096]{1,0:T(8,128)(2,1)} %tiles_hbm.1), custom_call_target="tpu_custom_call" | custom-call | tf_op jit(solution)/shard_map/block_sparse/pallas_call | solution.py:545
  48.3 0.6 %copy.8 = f32[8,2048]{1,0:T(8,128)} copy(f32[8,2048]{1,0:T(8,128)S(1)} %block_sparse.1) | data formatting | bytes 131072

commit v4 on v3

--- a/solution.py
+++ b/solution.py
@@ -113,28 +113,24 @@
         hot[block * 64 : (block + 1) * 64, :] = jnp.where(spots == ids, 1.0, 0.0).astype(jnp.bfloat16)
 
 
-def products(to, at, counts, tt, seg, terms, forward):
+def products(g, to, at, counts, tt, seg, terms, forward):
     n = counts[0, 0]
     high = (lax.broadcasted_iota(jnp.int32, (VECS, 128), 1) >= TILE).astype(jnp.int32)
 
-    def step(g, carry):
-        for u in range(UNROLL):
-            s = g * UNROLL + u
-            dead = ((s >= n).astype(jnp.int32)) * 2
-            given, wanted = at[s], to[s]
-            own = jnp.where(high == (given & 1) + dead, seg[given >> 1].astype(jnp.float32), 0.0)
-            if forward:
-                half = lax.dot_general(
-                    own.astype(jnp.bfloat16), tt[s], (((1,), (1,)), ((), ())), preferred_element_type=jnp.float32
-                )
-                both = jnp.concatenate([half, half], axis=1)
-            else:
-                own = (own + pltpu.roll(own, TILE, 1))[:, :TILE]
-                both = jnp.dot(own.astype(jnp.bfloat16), tt[s], preferred_element_type=jnp.float32)
-            terms[pl.ds(pl.multiple_of(s * VECS, VECS), VECS), :] = jnp.where(high == (wanted & 1), both, 0.0)
-        return carry
-
-    lax.fori_loop(0, SLOTS // UNROLL, step, 0)
+    for u in range(UNROLL):
+        s = g * UNROLL + u
+        dead = ((s >= n).astype(jnp.int32)) * 2
+        given, wanted = at[s], to[s]
+        own = jnp.where(high == (given & 1) + dead, seg[given >> 1].astype(jnp.float32), 0.0)
+        if forward:
+            half = lax.dot_general(
+                own.astype(jnp.bfloat16), tt[s], (((1,), (1,)), ((), ())), preferred_element_type=jnp.float32
+            )
+            both = jnp.concatenate([half, half], axis=1)
+        else:
+            own = (own + pltpu.roll(own, TILE, 1))[:, :TILE]
+            both = jnp.dot(own.astype(jnp.bfloat16), tt[s], preferred_element_type=jnp.float32)
+        terms[s * VECS : (s + 1) * VECS, :] = jnp.where(high == (wanted & 1), both, 0.0)
 
 
 def spread(terms, twins, hot, sums):
@@ -156,10 +152,10 @@
 
 
 def kernel(
-    cols, rows, counts, cols_vec, rows_vec, vec_hbm, tiles_hbm, out,
-    vec, col, row, tiles, tt, flat, woven, pair_hot, side_hot, terms, twins, pcol, prow,
+    cols_hbm, rows_hbm, counts, cols_flat, rows_flat, vec_hbm, tiles_hbm, out,
+    cols, rows, cols_vec, rows_vec, vec, col, row, tiles, tt, flat, woven, pair_hot, side_hot, terms, twins, pcol, prow,
     near_buf, tree_out, tree_buf, more_out, more_buf, side_out, side_buf,
-    near_send, tree_send, pass_send, col_recv, row_send, row_recv, own_sem, tile_sem, vec_sem,
+    near_send, tree_send, pass_send, col_recv, row_send, row_recv, own_sem, tile_sem, vec_sem, index_sem,
     near_out, near_in, tree_from, tree_into, more_from, more_into, side_from, side_into,
 ):
     r, c, zl, y, core, zh, x = place()
@@ -176,6 +172,12 @@
     greet(zl, y, core, zh, x)
     for copy in halves:
         copy.start()
+    lists = [
+        pltpu.make_async_copy(a, b, index_sem.at[n])
+        for n, (a, b) in enumerate(((cols_flat, cols_vec), (rows_flat, rows_vec), (cols_hbm, cols), (rows_hbm, rows)))
+    ]
+    for copy in lists:
+        copy.start()
 
     def prep(lo, hi):
         def one(g, carry):
@@ -225,10 +227,11 @@
     ]
     for copy in mine:
         copy.start()
-    halves[0].wait()
-    prep(0, 3)
-    halves[1].wait()
-    prep(3, 5)
+    for h in range(3):
+        halves[h].wait()
+        prep(3 * h, 3 * h + 3)
+    for copy in lists:
+        copy.wait()
     mark(pair_hot, cols_vec)
     mark(side_hot, rows_vec)
 
@@ -278,8 +281,8 @@
             push_col(p, pass_send.at[n], z_mate)
             near(n, p)
         round_side(0, 0)
-        halves[2].wait()
-        prep(5, 7)
+        halves[3].wait()
+        prep(9, 10)
         far_side()
         for n, d in ((5, 3), (6, -3)):
             p = ahead(d, zl)
@@ -287,23 +290,13 @@
             push_col(p, pass_send.at[n], z_mate)
             near(n, p)
         round_side(1, -way)
-        prep(7, 8)
+        prep(10, 11)
         p = ahead(4, zl)
         got_col(p)
         push_col(p, pass_send.at[7], z_mate)
         near(7, p)
         round_side(2, way)
-        prep(8, 9)
-        for n, d in enumerate((0, 2, -2)):
-            p = ahead(d, 1 - zl)
-            got_col(p)
-            near(8 + n, p)
-        halves[3].wait()
-        prep(9, 10)
-        for n, d in enumerate((1, -1, 3, -3, 4)):
-            p = ahead(d, 1 - zl)
-            got_col(p)
-            near(11 + n, p)
+        prep(11, 12)
 
     @pl.when(core == 1)
     def _():
@@ -320,8 +313,8 @@
             got_col(p)
             near(n, p)
         round_side(0, 0)
-        halves[2].wait()
-        prep(5, 7)
+        halves[3].wait()
+        prep(9, 10)
         far_side()
         p = ahead(-2, 1 - zl)
         got_col(p)
@@ -333,32 +326,24 @@
         push_col(q, pass_send.at[7], ahead(-1, zl))
         near(7, q)
         round_side(1, -way)
-        prep(7, 8)
-        for n, d in enumerate((3, -3, 4)):
-            p = ahead(d, zl)
-            got_col(p)
-            near(8 + n, p)
+        prep(10, 11)
         round_side(2, way)
-        prep(8, 9)
-        for n, d in enumerate((1, -1)):
-            p = ahead(d, 1 - zl)
-            got_col(p)
-            near(11 + n, p)
-        halves[3].wait()
-        prep(9, 10)
-        for n, d in enumerate((3, -3, 4)):
-            p = ahead(d, 1 - zl)
-            got_col(p)
-            near(13 + n, p)
-
-    prep(10, 12)
+        prep(11, 12)
+
     for copy in mine:
         copy.wait()
     for d in range(NZH):
         got_row(across(d, way))
         got_row(across(d, 2))
     got_row(across(2, -way))
-    products(cols, rows, counts, tt, row, terms, False)
+    last = zip(((0, 1), (2, 1), (-2, 1), (1, 1), (-1, 1), (3, 1), (-3, 1), (4, 1)),
+               ((3, 0), (-3, 0), (4, 0), (1, 1), (-1, 1), (3, 1), (-3, 1), (4, 1)))
+    for n, ((d0, z0), (d1, z1)) in enumerate(last):
+        p = ahead(d0 + core * (d1 - d0), (zl + z0 + core * (z1 - z0)) % 2)
+        got_col(p)
+        near(8 + n, p)
+        if n < SLOTS // UNROLL:
+            products(n, cols, rows, counts, tt, row, terms, False)
     spread(terms, twins, pair_hot, pcol)
 
     def rel(d):
@@ -375,8 +360,8 @@
     for z in (0, 1):
         for d in range(NY):
             got_col(row_id((zl + z) % 2, (y + d) % NY, 1 - core))
-    products(rows, cols, counts, tt, col, terms, True)
-    spread(terms, twins, side_hot, prow)
+    for n in range(SLOTS // UNROLL):
+        products(n, rows, cols, counts, tt, col, terms, True)
 
     tree = (tree_out, tree_buf, tree_from, tree_into)
     more = (more_out, more_buf, more_from, more_into)
@@ -457,65 +442,62 @@
     def row_minus():
         send(side_kind, 14, row_sum(1, -way), bcol=across(-way, 0))
 
+    def mine_of(d):
+        return pair(0, d)
+
+    def others(d):
+        return pair(1, d)
+
+    def crossed(d):
+        return take(more, rel(d), pair(0, d))
+
     @pl.when(core == 0)
     def _():
-
-        def cross(d):
+        for d in (4, -3, 3, -2, 2, -1, 1, 0):
             send(more, rel(d), pair(1, d), brow=z_mate)
 
-        def value(d):
-            return take(more, rel(d), pair(0, d))
-
+    @pl.when(core == 1)
+    def _():
+        outer(more, 1, others)
+        outer(tree, way, mine_of)
+
+    spread(terms, twins, side_hot, prow)
+
+    @pl.when(core == 0)
+    def _():
         row_out_two(1, -way)
-        cross(4)
-        cross(-3)
-        cross(3)
         row_out_two(2, way)
-        cross(-2)
-        cross(2)
+        outer(tree, way, crossed)
         row_far()
-        cross(-1)
-        cross(1)
+        row_out_two(3, 0)
+        inner(tree, way, crossed)
         row_out_one(1, -way)
-        cross(0)
+        row_out_one(2, way)
+        row_two()
+        middle(tree, way, crossed)
+        row_minus()
+        row_plus()
+        row_out_one(3, 0)
+        finish(row_total(gathered(tree, crossed(0))))
+
+    @pl.when(core == 1)
+    def _():
+        row_out_two(1, -way)
+        row_out_two(2, way)
+        row_far()
+        inner(more, 1, others)
+        middle(more, 1, others)
         row_out_two(3, 0)
-        outer(tree, way, value)
+        row_out_one(1, -way)
         row_out_one(2, way)
+        inner(tree, way, mine_of)
+        middle(tree, way, mine_of)
         row_two()
         row_minus()
         row_plus()
-        middle(tree, way, value)
+        send(more, 7, gathered(more, others(0)), brow=z_mate)
         row_out_one(3, 0)
-        inner(tree, way, value)
-        finish(row_total(gathered(tree, value(0))))
-
-    @pl.when(core == 1)
-    def _():
-
-        def mine(d):
-            return pair(0, d)
-
-        def others(d):
-            return pair(1, d)
-
-        row_out_two(1, -way)
-        outer(more, 1, others)
-        row_out_two(2, way)
-        outer(tree, way, mine)
-        row_far()
-        row_out_one(1, -way)
-        row_out_two(3, 0)
-        row_out_one(2, way)
-        middle(more, 1, others)
-        inner(more, 1, others)
-        row_two()
-        row_minus()
-        row_plus()
-        middle(tree, way, mine)
-        inner(tree, way, mine)
-        row_out_one(3, 0)
-        send(more, 7, gathered(more, others(0)), brow=z_mate)
-        finish(take(more, 7, row_total(gathered(tree, mine(0)))))
+        finish(take(more, 7, row_total(gathered(tree, mine_of(0)))))
 
     for n in range(16):
         remote(part(pcol, 0), near_buf.at[0], near_out.at[n], own_sem.at[0], brow=core_mate).wait_send()
@@ -545,10 +527,14 @@
     return pl.pallas_call(
         kernel,
         name="block_sparse",
-        in_specs=[smem, smem, smem, vmem, vmem, hbm, hbm],
+        in_specs=[hbm, hbm, smem, hbm, hbm, hbm, hbm],
         out_specs=vmem,
         out_shape=jax.ShapeDtypeStruct((VECS, PIECE), f32),
         scratch_shapes=[
+            pltpu.SMEM((SLOTS,), jnp.int32),
+            pltpu.SMEM((SLOTS,), jnp.int32),
+            pltpu.VMEM((1, SLOTS), jnp.int32),
+            pltpu.VMEM((1, SLOTS), jnp.int32),
             pltpu.VMEM((BLOCKS, VECS, 128), bf16),
             pltpu.VMEM((ROWS * BLOCKS, VECS, 128), bf16),
             pltpu.VMEM((COLS * BLOCKS, VECS, 128), bf16),
@@ -565,11 +551,11 @@
             pltpu.VMEM((16, BLOCKS * VECS, 128), f32),
             *wires(7), *wires(8), *wires(15),
         ]
-        + [dma((n,)) for n in (16, 7, 8, ROWS, 15, COLS, 3, 4, BLOCKS)]
+        + [dma((n,)) for n in (16, 7, 8, ROWS, 15, COLS, 3, 4, BLOCKS, 4)]
         + [dma((n,)) for n in (16, 16, 7, 7, 8, 8, 15, 15)],
         compiler_params=pltpu.CompilerParams(collective_id=0, has_side_effects=True, vmem_limit_bytes=VMEM),
     )(
-        far(tile_cols), far(tile_rows), counts, tile_cols.reshape(1, SLOTS), tile_rows.reshape(1, SLOTS),
+        far(tile_cols), far(tile_rows), counts, far(tile_cols.reshape(1, SLOTS)), far(tile_rows.reshape(1, SLOTS)),
         far(vectors), far(tiles),
     )
 

time: 49.7 us -> 47.1 us (0.948); the launches traced: 49 us -> 46.9 us
  Pallas kernels: 47.7 us -> 45.6 us
    pallas_call x1, Pallas kernels: 47.7 us -> 45.6 us  [body(): pl.pallas_call(kernel, name='block_sparse', in_specs=[hbm, hbm, smem, hbm...]
where the time goes in v4:
time: 47.1 us; the launch traced here: 46.9 us
  Pallas kernels  45.6 us (97%)
  between operations  0.66 us (1%)
  local copies, waits for them, and re-layouts  0.63 us (1%)
    pallas_call x1, Pallas kernels, body(): pl.pallas_call(kernel, name='block_sparse', in_specs=[hbm, hbm, smem, hbm...  45.6 us

profile of v4, /device:TPU:6, one launch (start us, length us, event | category | flops | bytes accessed | tf_op | source)
XLA Modules:
  0.0 46.9 jit_solution(9669285294450716329)
XLA Ops:
  0.7 45.6 %block_sparse.1 = f32[8,2048]{1,0:T(8,128)S(1)} custom-call(s32[192]{0:T(256)} %cols_hbm.1, s32[192]{0:T(256)} %rows_hbm.1, s32[1,1]{1,0:T(1,128)S(6)} %copy.7.counts, s32[1,192]{1,0:T(1,128)} %bitcast.2, s32[1,192]{1,0:T(1,128)} %bitcast.3, bf16[8,2048]{1,0:T(8,128)(2,1)} %vec_hbm.1, bf16[192,4096]{1,0:T(8,128)(2,1)} %tiles_hbm.1), custom_call_target="tpu_custom_call" | custom-call | tf_op jit(solution)/shard_map/block_sparse/pallas_call | solution.py:527
  46.3 0.6 %copy.8 = f32[8,2048]{1,0:T(8,128)} copy(f32[8,2048]{1,0:T(8,128)S(1)} %block_sparse.1) | data formatting | bytes 131072

commit v5 on v4

--- a/solution.py
+++ b/solution.py
@@ -15,8 +15,8 @@
 NY, NX, NZH = 8, 4, 4
 ROWS, COLS = 32, 16
 GROUP = 16
-UNROLL = 32
-SPAN = 128
+UNROLL = 64
+SPAN = 256
 WIRE = PIECE + 128
 FULL = 32000.0
 VMEM = 32 << 20

time: 47.1 us -> 46.1 us (0.979)
  Pallas kernels: 45.6 us -> 44.7 us
    pallas_call x1, Pallas kernels: 45.6 us -> 44.7 us  [body(): pl.pallas_call(kernel, name='block_sparse', in_specs=[hbm, hbm, smem, hbm...]
where the time goes in v5:
time: 46.1 us; the launch traced here: 46 us
  Pallas kernels  44.7 us (97%)
  between operations  0.66 us (1%)
  local copies, waits for them, and re-layouts  0.63 us (1%)
    pallas_call x1, Pallas kernels, body(): pl.pallas_call(kernel, name='block_sparse', in_specs=[hbm, hbm, smem, hbm...  44.7 us

profile of v5, /device:TPU:6, one launch (start us, length us, event | category | flops | bytes accessed | tf_op | source)
XLA Modules:
  0.0 46.0 jit_solution(17136386091545387066)
XLA Ops:
  0.7 44.7 %block_sparse.1 = f32[8,2048]{1,0:T(8,128)S(1)} custom-call(s32[192]{0:T(256)} %cols_hbm.1, s32[192]{0:T(256)} %rows_hbm.1, s32[1,1]{1,0:T(1,128)S(6)} %copy.7.counts, s32[1,192]{1,0:T(1,128)} %bitcast.2, s32[1,192]{1,0:T(1,128)} %bitcast.3, bf16[8,2048]{1,0:T(8,128)(2,1)} %vec_hbm.1, bf16[192,4096]{1,0:T(8,128)(2,1)} %tiles_hbm.1), custom_call_target="tpu_custom_call" | custom-call | tf_op jit(solution)/shard_map/block_sparse/pallas_call | solution.py:527
  45.3 0.6 %copy.8 = f32[8,2048]{1,0:T(8,128)} copy(f32[8,2048]{1,0:T(8,128)S(1)} %block_sparse.1) | data formatting | bytes 131072
